TPU v7x, 32 devices: a whole 2x2x4 slice. The times are simulated.
32 devices in a mesh: groups: 2 (over x), row: 16 (over z, y, core).
Axes of the slice: x: 2, y: 2, z: 4, core: 2. Of those that a mesh axis runs over, the one named last changes fastest.
Arguments:
- fine: bfloat16 [2048, 128, 128], P(('groups', 'row')), parts along dimension 0, may hold values from -6 to 6
- parent: bfloat16 [32, 256, 512], P(('groups', 'row')), parts along dimension 0, may hold values from -6 to 6
- coverage: int32 [64, 4], P('groups'), parts along dimension 0, may hold values from 0 to 15
- owner_slot: int32 [32], P('groups'), parts along dimension 0, may hold values from 0 to 15, each once
- w_query: bfloat16 [128, 128], replicated, may hold values from -0.5 to 0.5
- w_key: bfloat16 [512, 128], replicated, may hold values from -0.25 to 0.25
- w_value: bfloat16 [512, 128], replicated, may hold values from -0.25 to 0.25
- norm_gain: float32 [128], replicated, may hold values from 0.1 to 1.9
- conv_weight: bfloat16 [4, 3, 3, 128, 128], replicated, may hold values from -0.25 to 0.25
- conv_bias: float32 [4, 128], replicated, may hold values from -3 to 3
Outputs:
- refined: bfloat16 [2048, 128, 128], P(('groups', 'row')), parts along dimension 0
There are 2 independent parts, one for each index of `groups`. A program takes and returns all parts, laid end to end along the dimension named above; an argument that names none is the same for every part. Nothing has to cross between parts.
Inputs may be any that keep to these rules, and one draw needn't show every extreme that they name: `owner_slot`: each slot exactly once.
All inputs are finite; a program needn't handle non-finite values.
Results may differ from a plain program's by a relative error of at most 0.014.
Values may be sent and summed in bfloat16 or wider, within the bound.
No kernel may reach another device: no remote copies, remote signals or barrier semaphores. Data moves between devices by JAX's collectives and lax.ppermute only.
A program may use at most 128 MiB of HBM per device.

v0:
```python
import functools
import math

import jax
import jax.numpy as jnp
from jax import lax
from jax.experimental import pallas as pl
from jax.experimental.pallas import tpu as pltpu
from jax.sharding import PartitionSpec as P


BF16, F32 = jnp.bfloat16, jnp.float32
VMEM = pl.BlockSpec(memory_space=pltpu.VMEM)
SMEM = pl.BlockSpec(memory_space=pltpu.SMEM)
ANY = pl.BlockSpec(memory_space=pl.ANY)
HBM = pl.BlockSpec(memory_space=pltpu.HBM)
LARGE = 60 * 2**20
STEP = 16
GROUP = 18
SUB = 4


def encode_kernel(halo, parent_hbm, wk_hbm, wv_hbm, wq_hbm, fine_hbm, out_ref, inner_ref, outer_ref, *rest):
    parent_ref, wk_ref, wv_ref, wq_ref, sem = rest
    own = fine_hbm.shape[0]
    even = lax.rem(lax.axis_index("row"), 2) == 0
    plain = (
        (parent_hbm, parent_ref),
        (wk_hbm, wk_ref),
        (wv_hbm, wv_ref),
        (wq_hbm, wq_ref),
        (fine_hbm.at[pl.ds(jnp.where(even, own - halo, 0), halo)], inner_ref),
        (fine_hbm.at[pl.ds(jnp.where(even, 0, own - halo), halo)], outer_ref),
    )
    moves = [pltpu.make_async_copy(src, dst, sem.at[i]) for i, (src, dst) in enumerate(plain)]
    for move in moves:
        move.start()
    for move in moves[:4]:
        move.wait()
    rows, chans = parent_ref.shape[0], wk_ref.shape[1]
    parent = parent_ref[...]
    keys = jnp.dot(parent, wk_ref[...], preferred_element_type=F32)
    scale = math.log2(math.e) / math.sqrt(chans)
    folded = jnp.dot(wq_ref[...], keys.T.astype(BF16), preferred_element_type=F32) * scale
    values = jnp.dot(parent, wv_ref[...], preferred_element_type=F32).astype(BF16)
    out_ref[:chans, :] = folded.astype(BF16)
    for half in range(rows // chans):
        out_ref[chans:, half * chans : (half + 1) * chans] = values[half * chans : (half + 1) * chans]
    for move in moves[4:]:
        move.wait()


def encode(parent, w_key, w_value, w_query, fine, halo):
    rows, chans = parent.shape[0], w_key.shape[1]
    edge = jax.ShapeDtypeStruct((halo,) + fine.shape[1:], BF16)
    return pl.pallas_call(
        functools.partial(encode_kernel, halo),
        out_shape=[jax.ShapeDtypeStruct((2 * chans, rows), BF16), edge, edge],
        in_specs=[HBM] * 5,
        out_specs=[VMEM] * 3,
        scratch_shapes=[pltpu.VMEM(a.shape, a.dtype) for a in (parent, w_key, w_value, w_query)]
        + [pltpu.SemaphoreType.DMA((6,))],
        compiler_params=pltpu.CompilerParams(vmem_limit_bytes=LARGE),
        name="encode",
    )(parent, w_key, w_value, w_query, fine)


def ring_shape(count):
    per_chip = 2 if count % 2 == 0 else 1
    return per_chip, count // per_chip


def ring_place(chip, chips):
    half = lax.div(chip, 2)
    return jnp.where(lax.rem(chip, 2) == 0, half, chips - 1 - half)


def gather_blocks(block, count):
    per_chip, chips = ring_shape(count)
    order = list(range(0, chips, 2)) + list(range(1, chips, 2))[::-1]

    def step(array, shift):
        pairs = [
            (order[at] * per_chip + core, order[(at + shift) % chips] * per_chip + core)
            for at in range(chips)
            for core in range(per_chip)
        ]
        return lax.ppermute(array, "row", pairs)

    held = {0: block}
    ahead = behind = block
    up, down = chips // 2, (chips - 1) // 2
    for hop in range(1, up + 1):
        ahead = step(ahead, 1)
        held[chips - hop] = ahead
        if hop <= down:
            behind = step(behind, -1)
            held[hop] = behind
    own = [held[offset] for offset in range(chips)]
    if per_chip == 1:
        return own
    partner = [(i, i ^ 1) for i in range(count)]
    others = []
    for array in own:
        others.append(lax.ppermute(array, "row", partner))
    return own + others


def main_kernel(
    count, step, coverage_ref, owner_ref, fine_hbm, inner_hbm, outer_hbm, gain_hbm, kernel_hbm, bias_hbm, *rest
):
    blocks, out_hbm, rest = rest[:count], rest[count], rest[count + 1 :]
    cells, mixed, keys, values, scores, tops, gain_v, kernels, weight, bias_v, state_a, state_b = rest[:12]
    rows_f32, out, sem_kv, sem, sem_out = rest[12:]
    halo, own = inner_hbm.shape[0], fine_hbm.shape[0]
    cols, chans = cells.shape[1:]
    half = cols // 2
    tiles = coverage_ref.shape[0] // count
    cover = coverage_ref.shape[1]
    kv_rows = blocks[0].shape[1]
    layers = weight.shape[0]
    wide = cols // tiles
    per_chip, chips = ring_shape(count)
    position = lax.axis_index("row")
    home = ring_place(lax.div(position, per_chip), chips)
    core = lax.rem(position, per_chip)
    first, last = position == 0, position == count - 1
    even = lax.rem(position, 2) == 0

    plain = [
        (kernel_hbm, kernels),
        (fine_hbm, cells.at[halo : halo + own]),
        (gain_hbm, gain_v),
        (inner_hbm, cells.at[pl.ds(jnp.where(even, halo + own, 0), halo)]),
        (outer_hbm, cells.at[pl.ds(jnp.where(even, 0, halo + own), halo)]),
        (bias_hbm, bias_v),
    ]
    moves = [pltpu.make_async_copy(src, dst, sem.at[i]) for i, (src, dst) in enumerate(plain)]
    for move in moves[:3]:
        move.start()
    block_moves = []
    for at, ref in enumerate(blocks):
        block_moves.append(pltpu.make_async_copy(ref.at[0:chans], keys.at[at], sem_kv.at[at, 0]))
        for part in range(kv_rows // chans):
            block_moves.append(
                pltpu.make_async_copy(
                    ref.at[chans : 2 * chans, part * chans : (part + 1) * chans],
                    values.at[at, part * chans : (part + 1) * chans, 0:chans],
                    sem_kv.at[at, 1 + part],
                )
            )
    for move in block_moves + moves[3:]:
        move.start()
    values[:, :, chans:] = jnp.ones(values.shape[:2] + (values.shape[2] - chans,), BF16)

    def picks(level, tile):
        line = jnp.minimum(jnp.maximum(position + level, 0), count - 1)
        out = []
        for j in range(cover):
            slot = owner_ref[coverage_ref[line * tiles + tile, j]]
            offset = ring_place(lax.div(slot, per_chip), chips) - home
            offset = jnp.where(offset < 0, offset + chips, offset)
            out.append(jnp.where(lax.rem(slot, per_chip) == core, 0, chips) + offset)
        return out

    chosen = {(level, tile): picks(level, tile) for level in (0, -1, 1) for tile in range(tiles)}

    moves[0].wait()
    zero = jnp.zeros((chans, chans), BF16)

    @pl.loop(0, layers)
    def _(layer):
        for tap in range(3):
            west, centre, east = (kernels[layer, tap, shift].astype(F32) for shift in range(3))
            outer = west + east
            terms = (0.5 * west, 0.25 * (outer + centre), 0.25 * (outer - centre), 0.5 * east)
            for term, value in enumerate(terms):
                value = value.astype(BF16)
                for to in range(2):
                    row = tap + to
                    weight[layer, term, row * chans : (row + 1) * chans, to * chans : (to + 1) * chans] = value
        for term in range(4):
            weight[layer, term, 3 * chans :, :chans] = zero
            weight[layer, term, :chans, chans:] = zero

    for move in moves[1:3] + block_moves:
        move.wait()
    gain = gain_v[...]

    def score(slot, row, size, level, tile):
        amount = size * wide
        part = cells[pl.ds(row, size), tile * wide : (tile + 1) * wide, :].reshape(amount, chans)
        top = None
        for j, which in enumerate(chosen[level, tile]):
            found = jnp.dot(part, keys[which], preferred_element_type=F32)
            scores[slot, :amount, j * kv_rows : (j + 1) * kv_rows] = found
            for lane in range(0, kv_rows, 128):
                piece = found[:, lane : lane + 128]
                top = piece if top is None else jnp.maximum(top, piece)
        tops[slot, :amount] = jnp.broadcast_to(jnp.max(top, -1, keepdims=True), (amount, 128))

    def mix(slot, row, size, level, tile):
        amount = size * wide
        top = tops[slot, :amount]
        probs = [
            jnp.exp2(scores[slot, :amount, lane : lane + 128] - top).astype(BF16)
            for lane in range(0, cover * kv_rows, 128)
        ]
        covered = jnp.concatenate([values[which] for which in chosen[level, tile]], 0)
        summed = jnp.dot(jnp.concatenate(probs, -1), covered, preferred_element_type=F32)
        attended, mass = summed[:, :chans], summed[:, chans:]
        meansq = jnp.mean(attended * attended, -1, keepdims=True)
        part = cells[pl.ds(row, size), tile * wide : (tile + 1) * wide, :].reshape(amount, chans)
        total = part.astype(F32) + gain * attended * lax.rsqrt(meansq + 1e-6 * mass * mass)
        mixed[pl.ds(row, size), tile * wide : (tile + 1) * wide, :] = total.reshape(size, wide, chans)

    score(0, halo, step, 0, 0)

    @pl.loop(0, own // step - 1)
    def _(i):
        row = halo + i * step
        for tile in range(tiles):
            ahead = (tile + 1) % tiles
            score(ahead % 2, row + (step if ahead == 0 else 0), step, 0, ahead)
            mix(tile % 2, row, step, 0, tile)

    for move in moves[3:]:
        move.wait()
    pieces = [(halo + own - step, step, 0, tile) for tile in range(tiles)]
    pieces += [(0, halo, -1, tile) for tile in range(tiles)]
    pieces += [(halo + own, halo, 1, tile) for tile in range(tiles)]
    for at, piece in enumerate(pieces):
        if at + 1 < len(pieces):
            score((at + 1) % 2, *pieces[at + 1])
        mix(at % 2, *piece)

    @pl.when(first)
    def _():
        mixed[:halo] = jnp.zeros((halo, cols, chans), F32)

    @pl.when(last)
    def _():
        mixed[halo + own :] = jnp.zeros((halo, cols, chans), F32)

    def put(dst, pair, amount, even, odd):
        column = lax.rem(lax.broadcasted_iota(jnp.int32, (amount * half, 1), 0), half)
        before = jnp.where(column == 0, 0.0, pltpu.roll(odd, 1, 0))
        after = jnp.where(column == half - 1, 0.0, pltpu.roll(even, amount * half - 1, 0))
        for term, value in enumerate((before - odd, even + odd, odd - even, even - after)):
            dst[term, pl.ds(pair, amount)] = value.astype(BF16).reshape(amount, half, 2 * chans)

    pairs = (own + 2 * halo) // 2

    batch = 4 if pairs % 4 == 0 else 1

    @pl.loop(0, pairs // batch)
    def _(i):
        for pair in range(batch):
            even, odd = (
                jnp.concatenate(
                    [mixed.at[2 * (i * batch + pair) + k][pl.ds(side, half, stride=2), :] for k in range(2)], -1
                )
                for side in range(2)
            )
            put(state_a, i * batch + pair, 1, even, odd)

    source, target = state_a, state_b
    for layer in range(layers):
        pairs -= 1
        group = min(range(GROUP // 2, GROUP + 1), key=lambda size: (-(-pairs // size) * size, -size))
        final = layer == layers - 1
        bias = 0.5 * jnp.concatenate([bias_v[layer : layer + 1, :]] * 2, -1)

        def convolve(at, amount, spare):
            terms = []
            for term in range(4):
                taps = [source[term, pl.ds(at + lower, amount)].reshape(amount * half, 2 * chans) for lower in range(2)]
                terms.append(jnp.dot(jnp.concatenate(taps, -1), weight[layer, term], preferred_element_type=F32))
            centre = terms[1] + bias
            even = centre + terms[2] + terms[0]
            odd = centre - terms[2] - terms[3]
            even = even + even * jnp.tanh(even)
            odd = odd + odd * jnp.tanh(odd)
            if not final:
                put(target, at, amount, even, odd)
                return
            for k in range(amount):
                for side in range(2):
                    one = rows_f32.at[spare + 2 * k + side]
                    one[pl.ds(0, half, stride=2), :] = even[k * half : (k + 1) * half, side * chans : (side + 1) * chans]
                    one[pl.ds(1, half, stride=2), :] = odd[k * half : (k + 1) * half, side * chans : (side + 1) * chans]
            out[pl.ds(2 * at, 2 * amount)] = rows_f32[spare : spare + 2 * amount].astype(BF16)

        @pl.loop(0, pl.cdiv(pairs, group))
        def _(i):
            start = jnp.minimum(i * group, pairs - group)
            subs = -(-group // SUB)
            for sub in range(subs):
                low, high = sub * group // subs, (sub + 1) * group // subs
                convolve(start + low, high - low, 2 * low)
            if final and pairs % group == 0:
                part = pl.ds(2 * start, 2 * group)
                pltpu.make_async_copy(out.at[part], out_hbm.at[part], sem_out.at[i]).start()

        margin = layers - 1 - layer
        if margin:
            blank = jnp.zeros((4, half, chans), BF16)

            @pl.when(first)
            def _():
                for row in range(margin):
                    target[:, row // 2, :, (row % 2) * chans : (row % 2 + 1) * chans] = blank

            @pl.when(last)
            def _():
                for row in range(2 * pairs - margin, 2 * pairs):
                    target[:, row // 2, :, (row % 2) * chans : (row % 2 + 1) * chans] = blank

        source, target = target, source
    if pairs % group == 0:
        for i in range(pairs // group):
            part = slice(2 * i * group, 2 * (i + 1) * group)
            pltpu.make_async_copy(out.at[part], out_hbm.at[part], sem_out.at[i]).wait()
    else:
        move = pltpu.make_async_copy(out, out_hbm, sem_out.at[0])
        move.start()
        move.wait()


def attend_and_convolve(coverage, owner_slot, fine, inner, outer, gain, kernels, bias, blocks):
    own, cols, chans = fine.shape
    halo, count, cover = inner.shape[0], len(blocks), coverage.shape[1]
    tiles = coverage.shape[0] // count
    kv_rows = blocks[0].shape[1]
    amount = STEP * cols // tiles
    total = own + 2 * halo
    state = pltpu.VMEM((4, total // 2, cols // 2, 2 * chans), BF16)
    return pl.pallas_call(
        functools.partial(main_kernel, count, STEP),
        out_shape=jax.ShapeDtypeStruct(fine.shape, BF16),
        in_specs=[SMEM] * 2 + [HBM] * (6 + count),
        out_specs=HBM,
        scratch_shapes=[
            pltpu.VMEM((total, cols, chans), BF16),
            pltpu.VMEM((total, cols, chans), F32),
            pltpu.VMEM((count, chans, kv_rows), BF16),
            pltpu.VMEM((count, kv_rows, 2 * chans), BF16),
            pltpu.VMEM((2, amount, cover * kv_rows), F32),
            pltpu.VMEM((2, amount, 128), F32),
            pltpu.VMEM(gain.shape, F32),
            pltpu.VMEM(kernels.shape, BF16),
            pltpu.VMEM((kernels.shape[0], 4, 4 * chans, 2 * chans), BF16),
            pltpu.VMEM(bias.shape, F32),
            state,
            state,
            pltpu.VMEM((2 * GROUP, cols, chans), F32),
            pltpu.VMEM(fine.shape, BF16),
            pltpu.SemaphoreType.DMA((count, 1 + kv_rows // chans)),
            pltpu.SemaphoreType.DMA((6,)),
            pltpu.SemaphoreType.DMA((own // 2,)),
        ],
        compiler_params=pltpu.CompilerParams(vmem_limit_bytes=LARGE),
        name="attend_and_convolve",
    )(coverage, owner_slot, fine, inner, outer, gain, kernels, bias, *blocks)


def on_device(
    fine, parent, coverage, owner_slot, w_query, w_key, w_value, norm_gain, conv_weight, conv_bias
):
    count = lax.axis_size("row")
    block, inner, outer = encode(parent[0], w_key, w_value, w_query, fine, conv_weight.shape[0])
    swap = lambda array, low: lax.ppermute(
        array, "row", [pair for i in range(low, count - 1, 2) for pair in ((i, i + 1), (i + 1, i))]
    )
    inner = swap(inner, 0)
    outer = swap(outer, 1)
    blocks = gather_blocks(block, count)
    return attend_and_convolve(
        coverage, owner_slot, fine, inner, outer, norm_gain[None], conv_weight, conv_bias, blocks
    )


def solution(mesh):
    placed = (
        P(("groups", "row"), None, None),
        P(("groups", "row"), None, None),
        P("groups", None),
        P("groups"),
        P(),
        P(),
        P(),
        P(),
        P(),
        P(),
    )
    return jax.shard_map(
        on_device,
        mesh=mesh,
        in_specs=placed,
        out_specs=P(("groups", "row"), None, None),
        check_vma=False,
    )
```

profile of v0, /device:TPU:1, one launch (start us, length us, event | category | flops | bytes accessed | tf_op | source)
XLA Modules:
  0.0 61.4 jit_solution(12071964354216891078)
XLA Ops:
  0.0 2.4 %encode.1 = (bf16[256,256]{1,0:T(8,128)(2,1)}, bf16[4,128,128]{2,1,0:T(8,128)(2,1)}, bf16[4,128,128]{2,1,0:T(8,128)(2,1)}) custom-call(bf16[256,512]{1,0:T(8,128)(2,1)} %bitcast.2, bf16[512,128]{1,0:T(8,128)(2,1)} %wk_hbm.1, bf16[512,128]{1,0:T(8,128)(2,1)} %wv_hbm.1, bf16[128,128]{1,0:T(8,128)(2,1)} %wq_hbm.1, bf16[64,128,128]{2,1,0:T(8,128)(2,1)} %fine_hbm.3), custom_call_target="tpu_custom_call" | custom-call | tf_op jit(solution)/shard_map/encode/pallas_call | solution.py:56
  2.4 2.2 %collective-permute-start.5 = (bf16[256,256]{1,0:T(8,128)(2,1)}, bf16[256,256]{1,0:T(8,128)(2,1)S(1)}, u32[]{:S(2)}, u32[]{:S(2)}) collective-permute-start(bf16[256,256]{1,0:T(8,128)(2,1)} %get-tuple-element.10.rest_0_), channel_id=1, source_target_pairs={{0,4},{1,5},{4,8},{5,9},{8,12},{9,13},{12,14},{13,15},{14,10},{15,... | collective-permute-start | bytes 393224 | tf_op jit(solution)/shard_map/ppermute | solution.py:88
  4.5 0.0 collective-permute-start.2
  4.5 3.3 %collective-permute-done.5.rest_7_ = bf16[256,256]{1,0:T(8,128)(2,1)S(1)} collective-permute-done((bf16[256,256]{1,0:T(8,128)(2,1)}, bf16[256,256]{1,0:T(8,128)(2,1)S(1)}, u32[]{:S(2)}, u32[]{:S(2)}) %collective-permute-start.5) | collective-permute-done | bytes 131104 | tf_op jit(solution)/shard_map/ppermute | solution.py:88
  7.9 1.2 %collective-permute-start.6 = (bf16[256,256]{1,0:T(8,128)(2,1)S(1)}, bf16[256,256]{1,0:T(8,128)(2,1)S(1)}, u32[]{:S(2)}, u32[]{:S(2)}) collective-permute-start(bf16[256,256]{1,0:T(8,128)(2,1)S(1)} %collective-permute-done.5.rest_7_), channel_id=1, source_target_pairs={{0,4},{1,5},{4,8},{5,9},{8,12},{9,13},{12,14},{13,15},{14,10},{15,... | collective-permute-start | bytes 393224 | tf_op jit(solution)/shard_map/ppermute | solution.py:88
  9.1 1.8 %collective-permute-start = (bf16[4,128,128]{2,1,0:T(8,128)(2,1)}, bf16[4,128,128]{2,1,0:T(8,128)(2,1)S(1)}, u32[]{:S(2)}, u32[]{:S(2)}) collective-permute-start(bf16[4,128,128]{2,1,0:T(8,128)(2,1)} %get-tuple-element.8), channel_id=1, source_target_pairs={{0,1},{1,0},{2,3},{3,2},{4,5},{5,4},{6,7},{7,6},{8,9},{9,8},{10,11... | collective-permute-start | bytes 393224 | tf_op jit(solution)/shard_map/ppermute | solution.py:372
  10.9 1.9 %collective-permute-start.1 = (bf16[4,128,128]{2,1,0:T(8,128)(2,1)}, bf16[4,128,128]{2,1,0:T(8,128)(2,1)S(1)}, u32[]{:S(2)}, u32[]{:S(2)}) collective-permute-start(bf16[4,128,128]{2,1,0:T(8,128)(2,1)} %get-tuple-element.9), channel_id=1, source_target_pairs={{1,2},{2,1},{3,4},{4,3},{5,6},{6,5},{7,8},{8,7},{9,10},{10,9},{11,... | collective-permute-start | bytes 393224 | tf_op jit(solution)/shard_map/ppermute | solution.py:372
  12.9 0.0 collective-permute-done.2.rest_1_
  12.9 2.4 %collective-permute-start.3 = (bf16[256,256]{1,0:T(8,128)(2,1)S(1)}, bf16[256,256]{1,0:T(8,128)(2,1)S(1)}, u32[]{:S(2)}, u32[]{:S(2)}) collective-permute-start(bf16[256,256]{1,0:T(8,128)(2,1)S(1)} %collective-permute-done.2.rest_1_), channel_id=1, source_target_pairs={{0,2},{1,3},{4,0},{5,1},{8,4},{9,5},{12,8},{13,9},{14,12},{15,13},... | collective-permute-start | bytes 393224 | tf_op jit(solution)/shard_map/ppermute | solution.py:88
  15.3 0.0 collective-permute-done.6.rest_6_
  15.3 0.0 collective-permute-start.7
  15.3 0.6 collective-permute-start.9
  15.9 0.0 collective-permute-done.inner_hbm
  15.9 0.1 collective-permute-start.16
  16.0 1.4 %collective-permute-done.1.outer_hbm = bf16[4,128,128]{2,1,0:T(8,128)(2,1)S(1)} collective-permute-done((bf16[4,128,128]{2,1,0:T(8,128)(2,1)}, bf16[4,128,128]{2,1,0:T(8,128)(2,1)S(1)}, u32[]{:S(2)}, u32[]{:S(2)}) %collective-permute-start.1) | collective-permute-done | bytes 131104 | tf_op jit(solution)/shard_map/ppermute | solution.py:372
  17.4 2.2 %collective-permute-done.3.rest_2_ = bf16[256,256]{1,0:T(8,128)(2,1)S(1)} collective-permute-done((bf16[256,256]{1,0:T(8,128)(2,1)S(1)}, bf16[256,256]{1,0:T(8,128)(2,1)S(1)}, u32[]{:S(2)}, u32[]{:S(2)}) %collective-permute-start.3) | collective-permute-done | bytes 131104 | tf_op jit(solution)/shard_map/ppermute | solution.py:88
  19.6 2.2 %collective-permute-start.4 = (bf16[256,256]{1,0:T(8,128)(2,1)S(1)}, bf16[256,256]{1,0:T(8,128)(2,1)S(1)}, u32[]{:S(2)}, u32[]{:S(2)}) collective-permute-start(bf16[256,256]{1,0:T(8,128)(2,1)S(1)} %collective-permute-done.3.rest_2_), channel_id=1, source_target_pairs={{0,2},{1,3},{4,0},{5,1},{8,4},{9,5},{12,8},{13,9},{14,12},{15,13},... | collective-permute-start | bytes 393224 | tf_op jit(solution)/shard_map/ppermute | solution.py:88
  21.8 0.7 %collective-permute-start.15 = (bf16[256,256]{1,0:T(8,128)(2,1)S(1)}, bf16[256,256]{1,0:T(8,128)(2,1)S(1)}, u32[]{:S(2)}, u32[]{:S(2)}) collective-permute-start(bf16[256,256]{1,0:T(8,128)(2,1)S(1)} %collective-permute-done.6.rest_6_), channel_id=1, source_target_pairs={{0,1},{1,0},{2,3},{3,2},{4,5},{5,4},{6,7},{7,6},{8,9},{9,8},{10,11... | collective-permute-start | bytes 393224 | tf_op jit(solution)/shard_map/ppermute | solution.py:105
  22.5 0.1 collective-permute-start.11
  22.6 0.4 collective-permute-start.14
  23.0 1.2 %collective-permute-done.4.rest_3_ = bf16[256,256]{1,0:T(8,128)(2,1)S(1)} collective-permute-done((bf16[256,256]{1,0:T(8,128)(2,1)S(1)}, bf16[256,256]{1,0:T(8,128)(2,1)S(1)}, u32[]{:S(2)}, u32[]{:S(2)}) %collective-permute-start.4) | collective-permute-done | bytes 131104 | tf_op jit(solution)/shard_map/ppermute | solution.py:88
  24.3 1.2 %collective-permute-start.12 = (bf16[256,256]{1,0:T(8,128)(2,1)S(1)}, bf16[256,256]{1,0:T(8,128)(2,1)S(1)}, u32[]{:S(2)}, u32[]{:S(2)}) collective-permute-start(bf16[256,256]{1,0:T(8,128)(2,1)S(1)} %collective-permute-done.4.rest_3_), channel_id=1, source_target_pairs={{0,1},{1,0},{2,3},{3,2},{4,5},{5,4},{6,7},{7,6},{8,9},{9,8},{10,11... | collective-permute-start | bytes 393224 | tf_op jit(solution)/shard_map/ppermute | solution.py:105
  25.5 0.7 %collective-permute-done.8.rest_4_ = bf16[256,256]{1,0:T(8,128)(2,1)S(1)} collective-permute-done((bf16[256,256]{1,0:T(8,128)(2,1)S(1)}, bf16[256,256]{1,0:T(8,128)(2,1)S(1)}, u32[]{:S(2)}, u32[]{:S(2)}) %collective-permute-start.8) | collective-permute-done | bytes 131104 | tf_op jit(solution)/shard_map/ppermute | solution.py:88
  26.2 1.5 %collective-permute-start.13 = (bf16[256,256]{1,0:T(8,128)(2,1)S(1)}, bf16[256,256]{1,0:T(8,128)(2,1)S(1)}, u32[]{:S(2)}, u32[]{:S(2)}) collective-permute-start(bf16[256,256]{1,0:T(8,128)(2,1)S(1)} %collective-permute-done.8.rest_4_), channel_id=1, source_target_pairs={{0,1},{1,0},{2,3},{3,2},{4,5},{5,4},{6,7},{7,6},{8,9},{9,8},{10,11... | collective-permute-start | bytes 393224 | tf_op jit(solution)/shard_map/ppermute | solution.py:105
  27.7 0.7 %copy.11.coverage_ref = s32[32,4]{1,0:T(8,128)} copy(s32[32,4]{0,1:T(4,128)S(1)} %copy-done.17) | data formatting | bytes 1024 | tf_op args[2]
  28.4 0.2 collective-permute-done.13.rest_12_
  28.8 0.2 copy-done.12
  29.0 0.1 copy-done.13
  29.1 0.0 copy-done.14
  29.1 0.1 copy-done.15
  29.2 0.1 copy-done.16
  29.3 31.9 %attend_and_convolve.1 = bf16[64,128,128]{2,1,0:T(8,128)(2,1)} custom-call(s32[32,4]{1,0:T(8,128)} %copy.11.coverage_ref, s32[16]{0:T(128)} %owner_ref.1, bf16[64,128,128]{2,1,0:T(8,128)(2,1)} %fine_hbm.3, bf16[4,128,128]{2,1,0:T(8,128)(2,1)} %copy-done.3, bf16[4,128,128]{2,1,0:T(8,128)(2,1)} %copy-done.4, f32[1,128]{1,0:T(1,128)} %bitcast.3, ...), custom_call_target="tpu_custom_call" | custom-call | tf_op jit(solution)/shard_map/attend_and_convolve/pallas_call | solution.py:338
  (41 shorter events, 0.1 us)
Async XLA Ops:
  0.0 27.7 %copy-start.17 = (s32[32,4]{0,1:T(4,128)S(1)}, s32[32,4]{0,1:T(4,128)}, u32[]{:S(2)}) copy-start(s32[32,4]{0,1:T(4,128)} %param.12) | copy-start | bytes 1540
  2.4 5.5 %collective-permute-start.5 = (bf16[256,256]{1,0:T(8,128)(2,1)}, bf16[256,256]{1,0:T(8,128)(2,1)S(1)}, u32[]{:S(2)}, u32[]{:S(2)}) collective-permute-start(bf16[256,256]{1,0:T(8,128)(2,1)} %get-tuple-element.10.rest_0_), channel_id=1, source_target_pairs={{0,4},{1,5},{4,8},{5,9},{8,12},{9,13},{12,14},{13,15},{14,10},{15,... | collective-permute-start | bytes 393224 | tf_op jit(solution)/shard_map/ppermute | solution.py:88
  4.5 8.3 %collective-permute-start.2 = (bf16[256,256]{1,0:T(8,128)(2,1)}, bf16[256,256]{1,0:T(8,128)(2,1)S(1)}, u32[]{:S(2)}, u32[]{:S(2)}) collective-permute-start(bf16[256,256]{1,0:T(8,128)(2,1)} %get-tuple-element.10.rest_0_), channel_id=1, source_target_pairs={{0,2},{1,3},{4,0},{5,1},{8,4},{9,5},{12,8},{13,9},{14,12},{15,13},... | collective-permute-start | bytes 393224 | tf_op jit(solution)/shard_map/ppermute | solution.py:88
  7.9 20.8 %copy-start = (bf16[256,256]{1,0:T(8,128)(2,1)}, bf16[256,256]{1,0:T(8,128)(2,1)S(1)}, u32[]{:S(2)}) copy-start(bf16[256,256]{1,0:T(8,128)(2,1)S(1)} %collective-permute-done.5.rest_7_) | copy-start | bytes 393220
  7.9 7.4 %collective-permute-start.6 = (bf16[256,256]{1,0:T(8,128)(2,1)S(1)}, bf16[256,256]{1,0:T(8,128)(2,1)S(1)}, u32[]{:S(2)}, u32[]{:S(2)}) collective-permute-start(bf16[256,256]{1,0:T(8,128)(2,1)S(1)} %collective-permute-done.5.rest_7_), channel_id=1, source_target_pairs={{0,4},{1,5},{4,8},{5,9},{8,12},{9,13},{12,14},{13,15},{14,10},{15,... | collective-permute-start | bytes 393224 | tf_op jit(solution)/shard_map/ppermute | solution.py:88
  9.1 6.8 %collective-permute-start = (bf16[4,128,128]{2,1,0:T(8,128)(2,1)}, bf16[4,128,128]{2,1,0:T(8,128)(2,1)S(1)}, u32[]{:S(2)}, u32[]{:S(2)}) collective-permute-start(bf16[4,128,128]{2,1,0:T(8,128)(2,1)} %get-tuple-element.8), channel_id=1, source_target_pairs={{0,1},{1,0},{2,3},{3,2},{4,5},{5,4},{6,7},{7,6},{8,9},{9,8},{10,11... | collective-permute-start | bytes 393224 | tf_op jit(solution)/shard_map/ppermute | solution.py:372
  10.9 6.5 %collective-permute-start.1 = (bf16[4,128,128]{2,1,0:T(8,128)(2,1)}, bf16[4,128,128]{2,1,0:T(8,128)(2,1)S(1)}, u32[]{:S(2)}, u32[]{:S(2)}) collective-permute-start(bf16[4,128,128]{2,1,0:T(8,128)(2,1)} %get-tuple-element.9), channel_id=1, source_target_pairs={{1,2},{2,1},{3,4},{4,3},{5,6},{6,5},{7,8},{8,7},{9,10},{10,9},{11,... | collective-permute-start | bytes 393224 | tf_op jit(solution)/shard_map/ppermute | solution.py:372
  12.9 15.8 %copy-start.1 = (bf16[256,256]{1,0:T(8,128)(2,1)}, bf16[256,256]{1,0:T(8,128)(2,1)S(1)}, u32[]{:S(2)}) copy-start(bf16[256,256]{1,0:T(8,128)(2,1)S(1)} %collective-permute-done.2.rest_1_) | copy-start | bytes 393220
  12.9 6.7 %collective-permute-start.3 = (bf16[256,256]{1,0:T(8,128)(2,1)S(1)}, bf16[256,256]{1,0:T(8,128)(2,1)S(1)}, u32[]{:S(2)}, u32[]{:S(2)}) collective-permute-start(bf16[256,256]{1,0:T(8,128)(2,1)S(1)} %collective-permute-done.2.rest_1_), channel_id=1, source_target_pairs={{0,2},{1,3},{4,0},{5,1},{8,4},{9,5},{12,8},{13,9},{14,12},{15,13},... | collective-permute-start | bytes 393224 | tf_op jit(solution)/shard_map/ppermute | solution.py:88
  15.3 13.4 %copy-start.2 = (bf16[256,256]{1,0:T(8,128)(2,1)}, bf16[256,256]{1,0:T(8,128)(2,1)S(1)}, u32[]{:S(2)}) copy-start(bf16[256,256]{1,0:T(8,128)(2,1)S(1)} %collective-permute-done.6.rest_6_) | copy-start | bytes 393220
  15.3 6.5 %collective-permute-start.7 = (bf16[256,256]{1,0:T(8,128)(2,1)S(1)}, bf16[256,256]{1,0:T(8,128)(2,1)S(1)}, u32[]{:S(2)}, u32[]{:S(2)}) collective-permute-start(bf16[256,256]{1,0:T(8,128)(2,1)S(1)} %collective-permute-done.6.rest_6_), channel_id=1, source_target_pairs={{0,4},{1,5},{4,8},{5,9},{8,12},{9,13},{12,14},{13,15},{14,10},{15,... | collective-permute-start | bytes 393224 | tf_op jit(solution)/shard_map/ppermute | solution.py:88
  15.3 6.5 %collective-permute-start.9 = (bf16[256,256]{1,0:T(8,128)(2,1)}, bf16[256,256]{1,0:T(8,128)(2,1)S(1)}, u32[]{:S(2)}, u32[]{:S(2)}) collective-permute-start(bf16[256,256]{1,0:T(8,128)(2,1)} %get-tuple-element.10.rest_0_), channel_id=1, source_target_pairs={{0,1},{1,0},{2,3},{3,2},{4,5},{5,4},{6,7},{7,6},{8,9},{9,8},{10,11... | collective-permute-start | bytes 393224 | tf_op jit(solution)/shard_map/ppermute | solution.py:105
  15.9 12.8 %copy-start.3 = (bf16[4,128,128]{2,1,0:T(8,128)(2,1)}, bf16[4,128,128]{2,1,0:T(8,128)(2,1)S(1)}, u32[]{:S(2)}) copy-start(bf16[4,128,128]{2,1,0:T(8,128)(2,1)S(1)} %collective-permute-done.inner_hbm) | copy-start | bytes 393220
  15.9 6.6 %collective-permute-start.16 = (bf16[256,256]{1,0:T(8,128)(2,1)S(1)}, bf16[256,256]{1,0:T(8,128)(2,1)S(1)}, u32[]{:S(2)}, u32[]{:S(2)}) collective-permute-start(bf16[256,256]{1,0:T(8,128)(2,1)S(1)} %collective-permute-done.5.rest_7_), channel_id=1, source_target_pairs={{0,1},{1,0},{2,3},{3,2},{4,5},{5,4},{6,7},{7,6},{8,9},{9,8},{10,11... | collective-permute-start | bytes 393224 | tf_op jit(solution)/shard_map/ppermute | solution.py:105
  17.4 11.3 %copy-start.4 = (bf16[4,128,128]{2,1,0:T(8,128)(2,1)}, bf16[4,128,128]{2,1,0:T(8,128)(2,1)S(1)}, u32[]{:S(2)}) copy-start(bf16[4,128,128]{2,1,0:T(8,128)(2,1)S(1)} %collective-permute-done.1.outer_hbm) | copy-start | bytes 393220
  17.4 5.2 %collective-permute-start.10 = (bf16[256,256]{1,0:T(8,128)(2,1)S(1)}, bf16[256,256]{1,0:T(8,128)(2,1)S(1)}, u32[]{:S(2)}, u32[]{:S(2)}) collective-permute-start(bf16[256,256]{1,0:T(8,128)(2,1)S(1)} %collective-permute-done.2.rest_1_), channel_id=1, source_target_pairs={{0,1},{1,0},{2,3},{3,2},{4,5},{5,4},{6,7},{7,6},{8,9},{9,8},{10,11... | collective-permute-start | bytes 393224 | tf_op jit(solution)/shard_map/ppermute | solution.py:105
  19.6 9.1 %copy-start.5 = (bf16[256,256]{1,0:T(8,128)(2,1)}, bf16[256,256]{1,0:T(8,128)(2,1)S(1)}, u32[]{:S(2)}) copy-start(bf16[256,256]{1,0:T(8,128)(2,1)S(1)} %collective-permute-done.3.rest_2_) | copy-start | bytes 393220
  19.6 4.7 %collective-permute-start.4 = (bf16[256,256]{1,0:T(8,128)(2,1)S(1)}, bf16[256,256]{1,0:T(8,128)(2,1)S(1)}, u32[]{:S(2)}, u32[]{:S(2)}) collective-permute-start(bf16[256,256]{1,0:T(8,128)(2,1)S(1)} %collective-permute-done.3.rest_2_), channel_id=1, source_target_pairs={{0,2},{1,3},{4,0},{5,1},{8,4},{9,5},{12,8},{13,9},{14,12},{15,13},... | collective-permute-start | bytes 393224 | tf_op jit(solution)/shard_map/ppermute | solution.py:88
  21.8 6.9 %copy-start.6 = (bf16[256,256]{1,0:T(8,128)(2,1)}, bf16[256,256]{1,0:T(8,128)(2,1)S(1)}, u32[]{:S(2)}) copy-start(bf16[256,256]{1,0:T(8,128)(2,1)S(1)} %collective-permute-done.7.rest_5_) | copy-start | bytes 393220
  21.8 4.4 %collective-permute-start.8 = (bf16[256,256]{1,0:T(8,128)(2,1)S(1)}, bf16[256,256]{1,0:T(8,128)(2,1)S(1)}, u32[]{:S(2)}, u32[]{:S(2)}) collective-permute-start(bf16[256,256]{1,0:T(8,128)(2,1)S(1)} %collective-permute-done.7.rest_5_), channel_id=1, source_target_pairs={{0,4},{1,5},{4,8},{5,9},{8,12},{9,13},{12,14},{13,15},{14,10},{15,... | collective-permute-start | bytes 393224 | tf_op jit(solution)/shard_map/ppermute | solution.py:88
  21.8 6.9 %copy-start.7 = (bf16[256,256]{1,0:T(8,128)(2,1)}, bf16[256,256]{1,0:T(8,128)(2,1)S(1)}, u32[]{:S(2)}) copy-start(bf16[256,256]{1,0:T(8,128)(2,1)S(1)} %collective-permute-done.9.rest_8_) | copy-start | bytes 393220
  21.8 6.6 %collective-permute-start.15 = (bf16[256,256]{1,0:T(8,128)(2,1)S(1)}, bf16[256,256]{1,0:T(8,128)(2,1)S(1)}, u32[]{:S(2)}, u32[]{:S(2)}) collective-permute-start(bf16[256,256]{1,0:T(8,128)(2,1)S(1)} %collective-permute-done.6.rest_6_), channel_id=1, source_target_pairs={{0,1},{1,0},{2,3},{3,2},{4,5},{5,4},{6,7},{7,6},{8,9},{9,8},{10,11... | collective-permute-start | bytes 393224 | tf_op jit(solution)/shard_map/ppermute | solution.py:105
  22.5 6.2 %copy-start.8 = (bf16[256,256]{1,0:T(8,128)(2,1)}, bf16[256,256]{1,0:T(8,128)(2,1)S(1)}, u32[]{:S(2)}) copy-start(bf16[256,256]{1,0:T(8,128)(2,1)S(1)} %collective-permute-done.16.rest_15_) | copy-start | bytes 393220
  22.5 5.9 %collective-permute-start.11 = (bf16[256,256]{1,0:T(8,128)(2,1)S(1)}, bf16[256,256]{1,0:T(8,128)(2,1)S(1)}, u32[]{:S(2)}, u32[]{:S(2)}) collective-permute-start(bf16[256,256]{1,0:T(8,128)(2,1)S(1)} %collective-permute-done.3.rest_2_), channel_id=1, source_target_pairs={{0,1},{1,0},{2,3},{3,2},{4,5},{5,4},{6,7},{7,6},{8,9},{9,8},{10,11... | collective-permute-start | bytes 393224 | tf_op jit(solution)/shard_map/ppermute | solution.py:105
  22.6 6.1 %copy-start.9 = (bf16[256,256]{1,0:T(8,128)(2,1)}, bf16[256,256]{1,0:T(8,128)(2,1)S(1)}, u32[]{:S(2)}) copy-start(bf16[256,256]{1,0:T(8,128)(2,1)S(1)} %collective-permute-done.10.rest_9_) | copy-start | bytes 393220
  22.6 5.8 %collective-permute-start.14 = (bf16[256,256]{1,0:T(8,128)(2,1)S(1)}, bf16[256,256]{1,0:T(8,128)(2,1)S(1)}, u32[]{:S(2)}, u32[]{:S(2)}) collective-permute-start(bf16[256,256]{1,0:T(8,128)(2,1)S(1)} %collective-permute-done.7.rest_5_), channel_id=1, source_target_pairs={{0,1},{1,0},{2,3},{3,2},{4,5},{5,4},{6,7},{7,6},{8,9},{9,8},{10,11... | collective-permute-start | bytes 393224 | tf_op jit(solution)/shard_map/ppermute | solution.py:105
  24.3 4.5 %copy-start.10 = (bf16[256,256]{1,0:T(8,128)(2,1)}, bf16[256,256]{1,0:T(8,128)(2,1)S(1)}, u32[]{:S(2)}) copy-start(bf16[256,256]{1,0:T(8,128)(2,1)S(1)} %collective-permute-done.4.rest_3_) | copy-start | bytes 393220
  24.3 4.2 %collective-permute-start.12 = (bf16[256,256]{1,0:T(8,128)(2,1)S(1)}, bf16[256,256]{1,0:T(8,128)(2,1)S(1)}, u32[]{:S(2)}, u32[]{:S(2)}) collective-permute-start(bf16[256,256]{1,0:T(8,128)(2,1)S(1)} %collective-permute-done.4.rest_3_), channel_id=1, source_target_pairs={{0,1},{1,0},{2,3},{3,2},{4,5},{5,4},{6,7},{7,6},{8,9},{9,8},{10,11... | collective-permute-start | bytes 393224 | tf_op jit(solution)/shard_map/ppermute | solution.py:105
  26.2 2.6 %copy-start.11 = (bf16[256,256]{1,0:T(8,128)(2,1)}, bf16[256,256]{1,0:T(8,128)(2,1)S(1)}, u32[]{:S(2)}) copy-start(bf16[256,256]{1,0:T(8,128)(2,1)S(1)} %collective-permute-done.8.rest_4_) | copy-start | bytes 393220
  26.2 2.5 %collective-permute-start.13 = (bf16[256,256]{1,0:T(8,128)(2,1)S(1)}, bf16[256,256]{1,0:T(8,128)(2,1)S(1)}, u32[]{:S(2)}, u32[]{:S(2)}) collective-permute-start(bf16[256,256]{1,0:T(8,128)(2,1)S(1)} %collective-permute-done.8.rest_4_), channel_id=1, source_target_pairs={{0,1},{1,0},{2,3},{3,2},{4,5},{5,4},{6,7},{7,6},{8,9},{9,8},{10,11... | collective-permute-start | bytes 393224 | tf_op jit(solution)/shard_map/ppermute | solution.py:105
  28.4 0.7 %copy-start.14 = (bf16[256,256]{1,0:T(8,128)(2,1)}, bf16[256,256]{1,0:T(8,128)(2,1)S(1)}, u32[]{:S(2)}) copy-start(bf16[256,256]{1,0:T(8,128)(2,1)S(1)} %collective-permute-done.14.rest_13_) | copy-start | bytes 393220
  28.4 0.7 %copy-start.15 = (bf16[256,256]{1,0:T(8,128)(2,1)}, bf16[256,256]{1,0:T(8,128)(2,1)S(1)}, u32[]{:S(2)}) copy-start(bf16[256,256]{1,0:T(8,128)(2,1)S(1)} %collective-permute-done.12.rest_11_) | copy-start | bytes 393220
  (3 other events, 2.0 us)
where the time goes:
time: 62 us; the launch traced here: 61.4 us
  Pallas kernels  34.3 us (55%)
  starting transfers between devices  16.4 us (26%)
  waiting for transfers between devices  9.11 us (15%)
  local copies, waits for them, and re-layouts  1.28 us (2%)
    pallas_call x1, Pallas kernels, attend_and_convolve(): pl.pallas_call(functools.partial(main_kernel, count, STEP), out_shape=jax...  31.9 us
    ppermute x7, starting transfers between devices, step(): return lax.ppermute(array, 'row', pairs)  8 us
    ppermute x7, waiting for transfers between devices, step(): return lax.ppermute(array, 'row', pairs)  7.41 us
    ppermute x8, starting transfers between devices, gather_blocks(): others.append(lax.ppermute(array, 'row', partner))  4.66 us
    ppermute x2, starting transfers between devices, on_device(): lax.ppermute(array, 'row', [pair for i in range(low, count - 1, 2) for pa...  3.72 us
    pallas_call x1, Pallas kernels, encode(): pl.pallas_call(functools.partial(encode_kernel, halo), out_shape=[jax.Sha...  2.36 us
    ppermute x2, waiting for transfers between devices, on_device(): lax.ppermute(array, 'row', [pair for i in range(low, count - 1, 2) for pa...  1.44 us
    unnamed x37, local copies, waits for them, and re-layouts  1.28 us
  transfers between devices with their start and end apart: 17, of which 6 were waited for; matrix products, arithmetic and copies ran while one was open for 1% of the time, Pallas kernels for 0%

commit v1 on v0

--- a/solution.py
+++ b/solution.py
@@ -115,8 +115,8 @@
     halo, own = inner_hbm.shape[0], fine_hbm.shape[0]
     cols, chans = cells.shape[1:]
     half = cols // 2
-    tiles = coverage_ref.shape[0] // count
-    cover = coverage_ref.shape[1]
+    tiles = coverage_ref.shape[1] // count
+    cover = coverage_ref.shape[0]
     kv_rows = blocks[0].shape[1]
     layers = weight.shape[0]
     wide = cols // tiles
@@ -157,7 +157,7 @@
         line = jnp.minimum(jnp.maximum(position + level, 0), count - 1)
         out = []
         for j in range(cover):
-            slot = owner_ref[coverage_ref[line * tiles + tile, j]]
+            slot = owner_ref[coverage_ref[j, line * tiles + tile]]
             offset = ring_place(lax.div(slot, per_chip), chips) - home
             offset = jnp.where(offset < 0, offset + chips, offset)
             out.append(jnp.where(lax.rem(slot, per_chip) == core, 0, chips) + offset)
@@ -329,8 +329,8 @@
 
 def attend_and_convolve(coverage, owner_slot, fine, inner, outer, gain, kernels, bias, blocks):
     own, cols, chans = fine.shape
-    halo, count, cover = inner.shape[0], len(blocks), coverage.shape[1]
-    tiles = coverage.shape[0] // count
+    halo, count, cover = inner.shape[0], len(blocks), coverage.shape[0]
+    tiles = coverage.shape[1] // count
     kv_rows = blocks[0].shape[1]
     amount = STEP * cols // tiles
     total = own + 2 * halo
@@ -376,7 +376,7 @@
     outer = swap(outer, 1)
     blocks = gather_blocks(block, count)
     return attend_and_convolve(
-        coverage, owner_slot, fine, inner, outer, norm_gain[None], conv_weight, conv_bias, blocks
+        coverage.T, owner_slot, fine, inner, outer, norm_gain[None], conv_weight, conv_bias, blocks
     )
 
 

time: 62 us -> 61.7 us (level)
  local copies, waits for them, and re-layouts: 1.28 us -> 0.57 us
  waiting for transfers between devices: 9.11 us -> 9.78 us
    unnamed x37 -> x34, local copies, waits for them, and re-layouts: 1.28 us -> 0.57 us
    ppermute x8, waiting for transfers between devices: 0.26 us -> 0.94 us  [gather_blocks(): others.append(lax.ppermute(array, 'row', partner))]
  transfers between devices with their start and end apart: 17 -> 17, of which waited for: 6 -> 6; matrix products, arithmetic and copies ran while one was open for 1% -> 0% of each run, Pallas kernels for 0% -> 0%
where the time goes in v1:
time: 61.7 us; the launch traced here: 61.2 us
  Pallas kernels  34 us (55%)
  starting transfers between devices  16.4 us (27%)
  waiting for transfers between devices  9.78 us (16%)
    pallas_call x1, Pallas kernels, attend_and_convolve(): pl.pallas_call(functools.partial(main_kernel, count, STEP), out_shape=jax...  31.7 us
    ppermute x7, starting transfers between devices, step(): return lax.ppermute(array, 'row', pairs)  8 us
    ppermute x7, waiting for transfers between devices, step(): return lax.ppermute(array, 'row', pairs)  7.4 us
    ppermute x8, starting transfers between devices, gather_blocks(): others.append(lax.ppermute(array, 'row', partner))  4.68 us
    ppermute x2, starting transfers between devices, on_device(): lax.ppermute(array, 'row', [pair for i in range(low, count - 1, 2) for pa...  3.72 us
    pallas_call x1, Pallas kernels, encode(): pl.pallas_call(functools.partial(encode_kernel, halo), out_shape=[jax.Sha...  2.37 us
    ppermute x2, waiting for transfers between devices, on_device(): lax.ppermute(array, 'row', [pair for i in range(low, count - 1, 2) for pa...  1.44 us
  transfers between devices with their start and end apart: 17, of which 6 were waited for; matrix products, arithmetic and copies ran while one was open for 0% of the time, Pallas kernels for 0%

profile of v1, /device:TPU:1, one launch (start us, length us, event | category | flops | bytes accessed | tf_op | source)
XLA Modules:
  0.0 61.2 jit_solution(1021588817479255794)
XLA Ops:
  0.0 2.4 %encode.1 = (bf16[256,256]{1,0:T(8,128)(2,1)}, bf16[4,128,128]{2,1,0:T(8,128)(2,1)}, bf16[4,128,128]{2,1,0:T(8,128)(2,1)}) custom-call(bf16[256,512]{1,0:T(8,128)(2,1)} %bitcast.3, bf16[512,128]{1,0:T(8,128)(2,1)} %wk_hbm.1, bf16[512,128]{1,0:T(8,128)(2,1)} %wv_hbm.1, bf16[128,128]{1,0:T(8,128)(2,1)} %wq_hbm.1, bf16[64,128,128]{2,1,0:T(8,128)(2,1)} %fine_hbm.3), custom_call_target="tpu_custom_call" | custom-call | tf_op jit(solution)/shard_map/encode/pallas_call | solution.py:56
  2.4 2.2 %collective-permute-start.5 = (bf16[256,256]{1,0:T(8,128)(2,1)}, bf16[256,256]{1,0:T(8,128)(2,1)S(1)}, u32[]{:S(2)}, u32[]{:S(2)}) collective-permute-start(bf16[256,256]{1,0:T(8,128)(2,1)} %get-tuple-element.10.rest_0_), channel_id=1, source_target_pairs={{0,4},{1,5},{4,8},{5,9},{8,12},{9,13},{12,14},{13,15},{14,10},{15,... | collective-permute-start | bytes 393224 | tf_op jit(solution)/shard_map/ppermute | solution.py:88
  4.5 0.0 collective-permute-start.2
  4.6 3.3 %collective-permute-done.5.rest_7_ = bf16[256,256]{1,0:T(8,128)(2,1)S(1)} collective-permute-done((bf16[256,256]{1,0:T(8,128)(2,1)}, bf16[256,256]{1,0:T(8,128)(2,1)S(1)}, u32[]{:S(2)}, u32[]{:S(2)}) %collective-permute-start.5) | collective-permute-done | bytes 131104 | tf_op jit(solution)/shard_map/ppermute | solution.py:88
  7.9 1.2 %collective-permute-start.6 = (bf16[256,256]{1,0:T(8,128)(2,1)S(1)}, bf16[256,256]{1,0:T(8,128)(2,1)S(1)}, u32[]{:S(2)}, u32[]{:S(2)}) collective-permute-start(bf16[256,256]{1,0:T(8,128)(2,1)S(1)} %collective-permute-done.5.rest_7_), channel_id=1, source_target_pairs={{0,4},{1,5},{4,8},{5,9},{8,12},{9,13},{12,14},{13,15},{14,10},{15,... | collective-permute-start | bytes 393224 | tf_op jit(solution)/shard_map/ppermute | solution.py:88
  9.1 1.8 %collective-permute-start = (bf16[4,128,128]{2,1,0:T(8,128)(2,1)}, bf16[4,128,128]{2,1,0:T(8,128)(2,1)S(1)}, u32[]{:S(2)}, u32[]{:S(2)}) collective-permute-start(bf16[4,128,128]{2,1,0:T(8,128)(2,1)} %get-tuple-element.8), channel_id=1, source_target_pairs={{0,1},{1,0},{2,3},{3,2},{4,5},{5,4},{6,7},{7,6},{8,9},{9,8},{10,11... | collective-permute-start | bytes 393224 | tf_op jit(solution)/shard_map/ppermute | solution.py:372
  10.9 1.9 %collective-permute-start.1 = (bf16[4,128,128]{2,1,0:T(8,128)(2,1)}, bf16[4,128,128]{2,1,0:T(8,128)(2,1)S(1)}, u32[]{:S(2)}, u32[]{:S(2)}) collective-permute-start(bf16[4,128,128]{2,1,0:T(8,128)(2,1)} %get-tuple-element.9), channel_id=1, source_target_pairs={{1,2},{2,1},{3,4},{4,3},{5,6},{6,5},{7,8},{8,7},{9,10},{10,9},{11,... | collective-permute-start | bytes 393224 | tf_op jit(solution)/shard_map/ppermute | solution.py:372
  12.9 0.0 collective-permute-done.2.rest_1_
  12.9 2.4 %collective-permute-start.3 = (bf16[256,256]{1,0:T(8,128)(2,1)S(1)}, bf16[256,256]{1,0:T(8,128)(2,1)S(1)}, u32[]{:S(2)}, u32[]{:S(2)}) collective-permute-start(bf16[256,256]{1,0:T(8,128)(2,1)S(1)} %collective-permute-done.2.rest_1_), channel_id=1, source_target_pairs={{0,2},{1,3},{4,0},{5,1},{8,4},{9,5},{12,8},{13,9},{14,12},{15,13},... | collective-permute-start | bytes 393224 | tf_op jit(solution)/shard_map/ppermute | solution.py:88
  15.3 0.0 collective-permute-done.6.rest_6_
  15.3 0.6 %collective-permute-start.9 = (bf16[256,256]{1,0:T(8,128)(2,1)}, bf16[256,256]{1,0:T(8,128)(2,1)S(1)}, u32[]{:S(2)}, u32[]{:S(2)}) collective-permute-start(bf16[256,256]{1,0:T(8,128)(2,1)} %get-tuple-element.10.rest_0_), channel_id=1, source_target_pairs={{0,1},{1,0},{2,3},{3,2},{4,5},{5,4},{6,7},{7,6},{8,9},{9,8},{10,11... | collective-permute-start | bytes 393224 | tf_op jit(solution)/shard_map/ppermute | solution.py:105
  15.9 0.0 collective-permute-done.inner_hbm
  15.9 0.1 collective-permute-start.16
  16.0 1.4 %collective-permute-done.1.outer_hbm = bf16[4,128,128]{2,1,0:T(8,128)(2,1)S(1)} collective-permute-done((bf16[4,128,128]{2,1,0:T(8,128)(2,1)}, bf16[4,128,128]{2,1,0:T(8,128)(2,1)S(1)}, u32[]{:S(2)}, u32[]{:S(2)}) %collective-permute-start.1) | collective-permute-done | bytes 131104 | tf_op jit(solution)/shard_map/ppermute | solution.py:372
  17.4 2.2 %collective-permute-done.3.rest_2_ = bf16[256,256]{1,0:T(8,128)(2,1)S(1)} collective-permute-done((bf16[256,256]{1,0:T(8,128)(2,1)S(1)}, bf16[256,256]{1,0:T(8,128)(2,1)S(1)}, u32[]{:S(2)}, u32[]{:S(2)}) %collective-permute-start.3) | collective-permute-done | bytes 131104 | tf_op jit(solution)/shard_map/ppermute | solution.py:88
  19.6 2.2 %collective-permute-start.4 = (bf16[256,256]{1,0:T(8,128)(2,1)S(1)}, bf16[256,256]{1,0:T(8,128)(2,1)S(1)}, u32[]{:S(2)}, u32[]{:S(2)}) collective-permute-start(bf16[256,256]{1,0:T(8,128)(2,1)S(1)} %collective-permute-done.3.rest_2_), channel_id=1, source_target_pairs={{0,2},{1,3},{4,0},{5,1},{8,4},{9,5},{12,8},{13,9},{14,12},{15,13},... | collective-permute-start | bytes 393224 | tf_op jit(solution)/shard_map/ppermute | solution.py:88
  21.8 0.0 collective-permute-done.7.rest_5_
  21.8 0.0 collective-permute-done.9.rest_8_
  21.8 0.7 %collective-permute-start.15 = (bf16[256,256]{1,0:T(8,128)(2,1)S(1)}, bf16[256,256]{1,0:T(8,128)(2,1)S(1)}, u32[]{:S(2)}, u32[]{:S(2)}) collective-permute-start(bf16[256,256]{1,0:T(8,128)(2,1)S(1)} %collective-permute-done.6.rest_6_), channel_id=1, source_target_pairs={{0,1},{1,0},{2,3},{3,2},{4,5},{5,4},{6,7},{7,6},{8,9},{9,8},{10,11... | collective-permute-start | bytes 393224 | tf_op jit(solution)/shard_map/ppermute | solution.py:105
  22.5 0.1 collective-permute-start.11
  22.6 0.0 collective-permute-done.10.rest_9_
  22.6 0.4 collective-permute-start.14
  23.1 1.2 %collective-permute-done.4.rest_3_ = bf16[256,256]{1,0:T(8,128)(2,1)S(1)} collective-permute-done((bf16[256,256]{1,0:T(8,128)(2,1)S(1)}, bf16[256,256]{1,0:T(8,128)(2,1)S(1)}, u32[]{:S(2)}, u32[]{:S(2)}) %collective-permute-start.4) | collective-permute-done | bytes 131104 | tf_op jit(solution)/shard_map/ppermute | solution.py:88
  24.3 1.2 %collective-permute-start.12 = (bf16[256,256]{1,0:T(8,128)(2,1)S(1)}, bf16[256,256]{1,0:T(8,128)(2,1)S(1)}, u32[]{:S(2)}, u32[]{:S(2)}) collective-permute-start(bf16[256,256]{1,0:T(8,128)(2,1)S(1)} %collective-permute-done.4.rest_3_), channel_id=1, source_target_pairs={{0,1},{1,0},{2,3},{3,2},{4,5},{5,4},{6,7},{7,6},{8,9},{9,8},{10,11... | collective-permute-start | bytes 393224 | tf_op jit(solution)/shard_map/ppermute | solution.py:105
  25.5 0.7 %collective-permute-done.8.rest_4_ = bf16[256,256]{1,0:T(8,128)(2,1)S(1)} collective-permute-done((bf16[256,256]{1,0:T(8,128)(2,1)S(1)}, bf16[256,256]{1,0:T(8,128)(2,1)S(1)}, u32[]{:S(2)}, u32[]{:S(2)}) %collective-permute-start.8) | collective-permute-done | bytes 131104 | tf_op jit(solution)/shard_map/ppermute | solution.py:88
  26.2 1.5 %collective-permute-start.13 = (bf16[256,256]{1,0:T(8,128)(2,1)S(1)}, bf16[256,256]{1,0:T(8,128)(2,1)S(1)}, u32[]{:S(2)}, u32[]{:S(2)}) collective-permute-start(bf16[256,256]{1,0:T(8,128)(2,1)S(1)} %collective-permute-done.8.rest_4_), channel_id=1, source_target_pairs={{0,1},{1,0},{2,3},{3,2},{4,5},{5,4},{6,7},{7,6},{8,9},{9,8},{10,11... | collective-permute-start | bytes 393224 | tf_op jit(solution)/shard_map/ppermute | solution.py:105
  27.7 0.0 collective-permute-done.15.rest_14_
  27.7 0.0 collective-permute-done.11.rest_10_
  27.7 0.0 collective-permute-done.12.rest_11_
  27.8 0.9 %collective-permute-done.13.rest_12_ = bf16[256,256]{1,0:T(8,128)(2,1)S(1)} collective-permute-done((bf16[256,256]{1,0:T(8,128)(2,1)S(1)}, bf16[256,256]{1,0:T(8,128)(2,1)S(1)}, u32[]{:S(2)}, u32[]{:S(2)}) %collective-permute-start.13) | collective-permute-done | bytes 131104 | tf_op jit(solution)/shard_map/ppermute | solution.py:105
  28.8 0.5 copy-done.16
  29.3 31.7 %attend_and_convolve.1 = bf16[64,128,128]{2,1,0:T(8,128)(2,1)} custom-call(s32[4,32]{1,0:T(4,128)} %bitcast.4, s32[16]{0:T(128)} %owner_ref.1, bf16[64,128,128]{2,1,0:T(8,128)(2,1)} %fine_hbm.3, bf16[4,128,128]{2,1,0:T(8,128)(2,1)} %copy-done.3, bf16[4,128,128]{2,1,0:T(8,128)(2,1)} %copy-done.4, f32[1,128]{1,0:T(1,128)} %bitcast.5, ...), custom_call_target="tpu_custom_call" | custom-call | tf_op jit(solution)/shard_map/attend_and_convolve/pallas_call | solution.py:338
  (38 shorter events, 0.1 us)
Async XLA Ops:
  2.4 5.5 %collective-permute-start.5 = (bf16[256,256]{1,0:T(8,128)(2,1)}, bf16[256,256]{1,0:T(8,128)(2,1)S(1)}, u32[]{:S(2)}, u32[]{:S(2)}) collective-permute-start(bf16[256,256]{1,0:T(8,128)(2,1)} %get-tuple-element.10.rest_0_), channel_id=1, source_target_pairs={{0,4},{1,5},{4,8},{5,9},{8,12},{9,13},{12,14},{13,15},{14,10},{15,... | collective-permute-start | bytes 393224 | tf_op jit(solution)/shard_map/ppermute | solution.py:88
  4.5 8.3 %collective-permute-start.2 = (bf16[256,256]{1,0:T(8,128)(2,1)}, bf16[256,256]{1,0:T(8,128)(2,1)S(1)}, u32[]{:S(2)}, u32[]{:S(2)}) collective-permute-start(bf16[256,256]{1,0:T(8,128)(2,1)} %get-tuple-element.10.rest_0_), channel_id=1, source_target_pairs={{0,2},{1,3},{4,0},{5,1},{8,4},{9,5},{12,8},{13,9},{14,12},{15,13},... | collective-permute-start | bytes 393224 | tf_op jit(solution)/shard_map/ppermute | solution.py:88
  7.9 20.8 %copy-start = (bf16[256,256]{1,0:T(8,128)(2,1)}, bf16[256,256]{1,0:T(8,128)(2,1)S(1)}, u32[]{:S(2)}) copy-start(bf16[256,256]{1,0:T(8,128)(2,1)S(1)} %collective-permute-done.5.rest_7_) | copy-start | bytes 393220
  7.9 7.4 %collective-permute-start.6 = (bf16[256,256]{1,0:T(8,128)(2,1)S(1)}, bf16[256,256]{1,0:T(8,128)(2,1)S(1)}, u32[]{:S(2)}, u32[]{:S(2)}) collective-permute-start(bf16[256,256]{1,0:T(8,128)(2,1)S(1)} %collective-permute-done.5.rest_7_), channel_id=1, source_target_pairs={{0,4},{1,5},{4,8},{5,9},{8,12},{9,13},{12,14},{13,15},{14,10},{15,... | collective-permute-start | bytes 393224 | tf_op jit(solution)/shard_map/ppermute | solution.py:88
  9.1 6.8 %collective-permute-start = (bf16[4,128,128]{2,1,0:T(8,128)(2,1)}, bf16[4,128,128]{2,1,0:T(8,128)(2,1)S(1)}, u32[]{:S(2)}, u32[]{:S(2)}) collective-permute-start(bf16[4,128,128]{2,1,0:T(8,128)(2,1)} %get-tuple-element.8), channel_id=1, source_target_pairs={{0,1},{1,0},{2,3},{3,2},{4,5},{5,4},{6,7},{7,6},{8,9},{9,8},{10,11... | collective-permute-start | bytes 393224 | tf_op jit(solution)/shard_map/ppermute | solution.py:372
  10.9 6.5 %collective-permute-start.1 = (bf16[4,128,128]{2,1,0:T(8,128)(2,1)}, bf16[4,128,128]{2,1,0:T(8,128)(2,1)S(1)}, u32[]{:S(2)}, u32[]{:S(2)}) collective-permute-start(bf16[4,128,128]{2,1,0:T(8,128)(2,1)} %get-tuple-element.9), channel_id=1, source_target_pairs={{1,2},{2,1},{3,4},{4,3},{5,6},{6,5},{7,8},{8,7},{9,10},{10,9},{11,... | collective-permute-start | bytes 393224 | tf_op jit(solution)/shard_map/ppermute | solution.py:372
  12.9 15.8 %copy-start.1 = (bf16[256,256]{1,0:T(8,128)(2,1)}, bf16[256,256]{1,0:T(8,128)(2,1)S(1)}, u32[]{:S(2)}) copy-start(bf16[256,256]{1,0:T(8,128)(2,1)S(1)} %collective-permute-done.2.rest_1_) | copy-start | bytes 393220
  12.9 6.7 %collective-permute-start.3 = (bf16[256,256]{1,0:T(8,128)(2,1)S(1)}, bf16[256,256]{1,0:T(8,128)(2,1)S(1)}, u32[]{:S(2)}, u32[]{:S(2)}) collective-permute-start(bf16[256,256]{1,0:T(8,128)(2,1)S(1)} %collective-permute-done.2.rest_1_), channel_id=1, source_target_pairs={{0,2},{1,3},{4,0},{5,1},{8,4},{9,5},{12,8},{13,9},{14,12},{15,13},... | collective-permute-start | bytes 393224 | tf_op jit(solution)/shard_map/ppermute | solution.py:88
  15.3 13.4 %copy-start.2 = (bf16[256,256]{1,0:T(8,128)(2,1)}, bf16[256,256]{1,0:T(8,128)(2,1)S(1)}, u32[]{:S(2)}) copy-start(bf16[256,256]{1,0:T(8,128)(2,1)S(1)} %collective-permute-done.6.rest_6_) | copy-start | bytes 393220
  15.3 6.5 %collective-permute-start.7 = (bf16[256,256]{1,0:T(8,128)(2,1)S(1)}, bf16[256,256]{1,0:T(8,128)(2,1)S(1)}, u32[]{:S(2)}, u32[]{:S(2)}) collective-permute-start(bf16[256,256]{1,0:T(8,128)(2,1)S(1)} %collective-permute-done.6.rest_6_), channel_id=1, source_target_pairs={{0,4},{1,5},{4,8},{5,9},{8,12},{9,13},{12,14},{13,15},{14,10},{15,... | collective-permute-start | bytes 393224 | tf_op jit(solution)/shard_map/ppermute | solution.py:88
  15.3 6.5 %collective-permute-start.9 = (bf16[256,256]{1,0:T(8,128)(2,1)}, bf16[256,256]{1,0:T(8,128)(2,1)S(1)}, u32[]{:S(2)}, u32[]{:S(2)}) collective-permute-start(bf16[256,256]{1,0:T(8,128)(2,1)} %get-tuple-element.10.rest_0_), channel_id=1, source_target_pairs={{0,1},{1,0},{2,3},{3,2},{4,5},{5,4},{6,7},{7,6},{8,9},{9,8},{10,11... | collective-permute-start | bytes 393224 | tf_op jit(solution)/shard_map/ppermute | solution.py:105
  15.9 12.8 %copy-start.3 = (bf16[4,128,128]{2,1,0:T(8,128)(2,1)}, bf16[4,128,128]{2,1,0:T(8,128)(2,1)S(1)}, u32[]{:S(2)}) copy-start(bf16[4,128,128]{2,1,0:T(8,128)(2,1)S(1)} %collective-permute-done.inner_hbm) | copy-start | bytes 393220
  15.9 6.6 %collective-permute-start.16 = (bf16[256,256]{1,0:T(8,128)(2,1)S(1)}, bf16[256,256]{1,0:T(8,128)(2,1)S(1)}, u32[]{:S(2)}, u32[]{:S(2)}) collective-permute-start(bf16[256,256]{1,0:T(8,128)(2,1)S(1)} %collective-permute-done.5.rest_7_), channel_id=1, source_target_pairs={{0,1},{1,0},{2,3},{3,2},{4,5},{5,4},{6,7},{7,6},{8,9},{9,8},{10,11... | collective-permute-start | bytes 393224 | tf_op jit(solution)/shard_map/ppermute | solution.py:105
  17.4 11.3 %copy-start.4 = (bf16[4,128,128]{2,1,0:T(8,128)(2,1)}, bf16[4,128,128]{2,1,0:T(8,128)(2,1)S(1)}, u32[]{:S(2)}) copy-start(bf16[4,128,128]{2,1,0:T(8,128)(2,1)S(1)} %collective-permute-done.1.outer_hbm) | copy-start | bytes 393220
  17.4 5.2 %collective-permute-start.10 = (bf16[256,256]{1,0:T(8,128)(2,1)S(1)}, bf16[256,256]{1,0:T(8,128)(2,1)S(1)}, u32[]{:S(2)}, u32[]{:S(2)}) collective-permute-start(bf16[256,256]{1,0:T(8,128)(2,1)S(1)} %collective-permute-done.2.rest_1_), channel_id=1, source_target_pairs={{0,1},{1,0},{2,3},{3,2},{4,5},{5,4},{6,7},{7,6},{8,9},{9,8},{10,11... | collective-permute-start | bytes 393224 | tf_op jit(solution)/shard_map/ppermute | solution.py:105
  19.6 9.1 %copy-start.5 = (bf16[256,256]{1,0:T(8,128)(2,1)}, bf16[256,256]{1,0:T(8,128)(2,1)S(1)}, u32[]{:S(2)}) copy-start(bf16[256,256]{1,0:T(8,128)(2,1)S(1)} %collective-permute-done.3.rest_2_) | copy-start | bytes 393220
  19.6 4.7 %collective-permute-start.4 = (bf16[256,256]{1,0:T(8,128)(2,1)S(1)}, bf16[256,256]{1,0:T(8,128)(2,1)S(1)}, u32[]{:S(2)}, u32[]{:S(2)}) collective-permute-start(bf16[256,256]{1,0:T(8,128)(2,1)S(1)} %collective-permute-done.3.rest_2_), channel_id=1, source_target_pairs={{0,2},{1,3},{4,0},{5,1},{8,4},{9,5},{12,8},{13,9},{14,12},{15,13},... | collective-permute-start | bytes 393224 | tf_op jit(solution)/shard_map/ppermute | solution.py:88
  21.8 6.9 %copy-start.6 = (bf16[256,256]{1,0:T(8,128)(2,1)}, bf16[256,256]{1,0:T(8,128)(2,1)S(1)}, u32[]{:S(2)}) copy-start(bf16[256,256]{1,0:T(8,128)(2,1)S(1)} %collective-permute-done.7.rest_5_) | copy-start | bytes 393220
  21.8 4.4 %collective-permute-start.8 = (bf16[256,256]{1,0:T(8,128)(2,1)S(1)}, bf16[256,256]{1,0:T(8,128)(2,1)S(1)}, u32[]{:S(2)}, u32[]{:S(2)}) collective-permute-start(bf16[256,256]{1,0:T(8,128)(2,1)S(1)} %collective-permute-done.7.rest_5_), channel_id=1, source_target_pairs={{0,4},{1,5},{4,8},{5,9},{8,12},{9,13},{12,14},{13,15},{14,10},{15,... | collective-permute-start | bytes 393224 | tf_op jit(solution)/shard_map/ppermute | solution.py:88
  21.8 6.9 %copy-start.7 = (bf16[256,256]{1,0:T(8,128)(2,1)}, bf16[256,256]{1,0:T(8,128)(2,1)S(1)}, u32[]{:S(2)}) copy-start(bf16[256,256]{1,0:T(8,128)(2,1)S(1)} %collective-permute-done.9.rest_8_) | copy-start | bytes 393220
  21.8 5.9 %collective-permute-start.15 = (bf16[256,256]{1,0:T(8,128)(2,1)S(1)}, bf16[256,256]{1,0:T(8,128)(2,1)S(1)}, u32[]{:S(2)}, u32[]{:S(2)}) collective-permute-start(bf16[256,256]{1,0:T(8,128)(2,1)S(1)} %collective-permute-done.6.rest_6_), channel_id=1, source_target_pairs={{0,1},{1,0},{2,3},{3,2},{4,5},{5,4},{6,7},{7,6},{8,9},{9,8},{10,11... | collective-permute-start | bytes 393224 | tf_op jit(solution)/shard_map/ppermute | solution.py:105
  22.5 6.2 %copy-start.8 = (bf16[256,256]{1,0:T(8,128)(2,1)}, bf16[256,256]{1,0:T(8,128)(2,1)S(1)}, u32[]{:S(2)}) copy-start(bf16[256,256]{1,0:T(8,128)(2,1)S(1)} %collective-permute-done.16.rest_15_) | copy-start | bytes 393220
  22.5 5.2 %collective-permute-start.11 = (bf16[256,256]{1,0:T(8,128)(2,1)S(1)}, bf16[256,256]{1,0:T(8,128)(2,1)S(1)}, u32[]{:S(2)}, u32[]{:S(2)}) collective-permute-start(bf16[256,256]{1,0:T(8,128)(2,1)S(1)} %collective-permute-done.3.rest_2_), channel_id=1, source_target_pairs={{0,1},{1,0},{2,3},{3,2},{4,5},{5,4},{6,7},{7,6},{8,9},{9,8},{10,11... | collective-permute-start | bytes 393224 | tf_op jit(solution)/shard_map/ppermute | solution.py:105
  22.6 6.1 %copy-start.9 = (bf16[256,256]{1,0:T(8,128)(2,1)}, bf16[256,256]{1,0:T(8,128)(2,1)S(1)}, u32[]{:S(2)}) copy-start(bf16[256,256]{1,0:T(8,128)(2,1)S(1)} %collective-permute-done.10.rest_9_) | copy-start | bytes 393220
  22.6 5.1 %collective-permute-start.14 = (bf16[256,256]{1,0:T(8,128)(2,1)S(1)}, bf16[256,256]{1,0:T(8,128)(2,1)S(1)}, u32[]{:S(2)}, u32[]{:S(2)}) collective-permute-start(bf16[256,256]{1,0:T(8,128)(2,1)S(1)} %collective-permute-done.7.rest_5_), channel_id=1, source_target_pairs={{0,1},{1,0},{2,3},{3,2},{4,5},{5,4},{6,7},{7,6},{8,9},{9,8},{10,11... | collective-permute-start | bytes 393224 | tf_op jit(solution)/shard_map/ppermute | solution.py:105
  24.3 4.5 %copy-start.10 = (bf16[256,256]{1,0:T(8,128)(2,1)}, bf16[256,256]{1,0:T(8,128)(2,1)S(1)}, u32[]{:S(2)}) copy-start(bf16[256,256]{1,0:T(8,128)(2,1)S(1)} %collective-permute-done.4.rest_3_) | copy-start | bytes 393220
  24.3 3.5 %collective-permute-start.12 = (bf16[256,256]{1,0:T(8,128)(2,1)S(1)}, bf16[256,256]{1,0:T(8,128)(2,1)S(1)}, u32[]{:S(2)}, u32[]{:S(2)}) collective-permute-start(bf16[256,256]{1,0:T(8,128)(2,1)S(1)} %collective-permute-done.4.rest_3_), channel_id=1, source_target_pairs={{0,1},{1,0},{2,3},{3,2},{4,5},{5,4},{6,7},{7,6},{8,9},{9,8},{10,11... | collective-permute-start | bytes 393224 | tf_op jit(solution)/shard_map/ppermute | solution.py:105
  26.2 2.6 %copy-start.11 = (bf16[256,256]{1,0:T(8,128)(2,1)}, bf16[256,256]{1,0:T(8,128)(2,1)S(1)}, u32[]{:S(2)}) copy-start(bf16[256,256]{1,0:T(8,128)(2,1)S(1)} %collective-permute-done.8.rest_4_) | copy-start | bytes 393220
  26.2 2.5 %collective-permute-start.13 = (bf16[256,256]{1,0:T(8,128)(2,1)S(1)}, bf16[256,256]{1,0:T(8,128)(2,1)S(1)}, u32[]{:S(2)}, u32[]{:S(2)}) collective-permute-start(bf16[256,256]{1,0:T(8,128)(2,1)S(1)} %collective-permute-done.8.rest_4_), channel_id=1, source_target_pairs={{0,1},{1,0},{2,3},{3,2},{4,5},{5,4},{6,7},{7,6},{8,9},{9,8},{10,11... | collective-permute-start | bytes 393224 | tf_op jit(solution)/shard_map/ppermute | solution.py:105
  27.7 1.1 %copy-start.12 = (bf16[256,256]{1,0:T(8,128)(2,1)}, bf16[256,256]{1,0:T(8,128)(2,1)S(1)}, u32[]{:S(2)}) copy-start(bf16[256,256]{1,0:T(8,128)(2,1)S(1)} %collective-permute-done.15.rest_14_) | copy-start | bytes 393220
  27.7 1.1 %copy-start.13 = (bf16[256,256]{1,0:T(8,128)(2,1)}, bf16[256,256]{1,0:T(8,128)(2,1)S(1)}, u32[]{:S(2)}) copy-start(bf16[256,256]{1,0:T(8,128)(2,1)S(1)} %collective-permute-done.11.rest_10_) | copy-start | bytes 393220
  27.7 1.1 %copy-start.14 = (bf16[256,256]{1,0:T(8,128)(2,1)}, bf16[256,256]{1,0:T(8,128)(2,1)S(1)}, u32[]{:S(2)}) copy-start(bf16[256,256]{1,0:T(8,128)(2,1)S(1)} %collective-permute-done.14.rest_13_) | copy-start | bytes 393220
  (2 other events, 1.7 us)
